TPU v7x, 32 devices: a whole 2x2x4 slice. The times are simulated.
32 devices in a mesh: mem: 4 (over z), space: 8 (over y, x, core).
Axes of the slice: x: 2, y: 2, z: 4, core: 2. Of those that a mesh axis runs over, the one named last changes fastest.
Arguments:
- ensemble: float32 [128, 16, 2048], P('mem', 'space'), may hold values from -6 to 6
- forcing: float32 [16, 2048], P('space'), may hold values from 2 to 8
- obs_cell: int32 [1024], P('space'), may hold values from 0 to 32767, as said below
- obs_value: float32 [1024], P('space'), may hold values from -8 to 8
- obs_var: float32 [1024], P('space'), may hold values from 0.5 to 2
- obs_noise: float32 [128, 1024], P('mem', 'space'), may hold values from -5 to 5
Outputs:
- analysis: float32 [128, 16, 2048], P('mem', 'space')
Inputs may be any that keep to these rules, and one draw needn't show every extreme that they name: `obs_cell`: entries 128 * s to 128 * (s + 1) - 1 name cells of planes 2 * s to 2 * (s + 1) - 1, a cell of plane x and position p having index x * 2048 + p.
All inputs are finite; a program needn't handle non-finite values.
Results may differ from a plain program's by a relative error of at most 0.00018.
Values sent between devices are 32-bit elements; how exact they have to be, the bound alone decides.
No kernel may reach another device: no remote copies, remote signals or barrier semaphores. Data moves between devices by JAX's collectives and lax.ppermute only.
A program may use at most 64 MiB of HBM per device.

v0:
```python
import jax
import jax.numpy as jnp
from jax import lax
from jax.sharding import PartitionSpec as P

FSTEPS = 4
ITERS = 6
time_step = 0.05
highest = lax.Precision.HIGHEST


def from_behind(value, axis, steps):
    count = lax.axis_size(axis)
    pairs = [(source, (source + steps) % count) for source in range(count)]
    return lax.ppermute(value, axis, pairs)


def padded_2(x, sides, width):
    for axis, dim in sides:
        size, length = (lax.axis_size(axis), x.shape[dim])
        up = [(i, (i + 1) % size) for i in range(size)]
        down = [(j, i) for i, j in up]
        last = lax.slice_in_dim(x, length - width, length, axis=dim)
        initial = lax.slice_in_dim(x, 0, width, axis=dim)
        before = lax.ppermute(last, axis, up)
        after = lax.ppermute(initial, axis, down)
        x = jnp.concatenate([before, x, after], axis=dim)
    return x


def taper_of(planes_a, planes_b, planes_all, reach_planes):
    spread = jnp.abs(planes_a[:, None] - planes_b[None, :])
    spread = jnp.minimum(spread, planes_all - spread)
    return jnp.maximum(0.0, 1.0 - spread.astype(jnp.float32) / reach_planes)


def collect_band(values, along, reach_slabs, mover):
    pieces = []
    for offset in range(-reach_slabs, reach_slabs + 1):
        if offset == 0:
            pieces.append(values)
        else:
            pieces.append(mover(values, -offset))
    return jnp.concatenate(pieces, axis=along)


def move_obs(values, amount):
    return from_behind(values, "space", amount)


def move_directions(values, amount):
    return from_behind(values, "space", amount)


def move_weights(values, amount):
    return from_behind(values, "space", amount)


def shards(ensemble, forcing, obs_cell, obs_value, obs_var, obs_noise):
    members_dev, planes_dev, plane_cells = ensemble.shape
    obs_dev = obs_cell.shape[0]
    space_count = lax.axis_size("space")
    mem_count = lax.axis_size("mem")
    space_index = lax.axis_index("space")
    mem_index = lax.axis_index("mem")
    members = members_dev * mem_count
    planes_all = planes_dev * space_count
    reach_slabs = min(8, space_count // 4)
    reach_planes = planes_dev * reach_slabs
    band_width = reach_slabs * obs_dev
    states = ensemble
    for counter in range(FSTEPS):
        padded = padded_2(states, (("space", 1),), 2)
        forward_one = padded[:, 3 : 3 + planes_dev]
        back_one = padded[:, 1 : 1 + planes_dev]
        back_two = padded[:, 0:planes_dev]
        states = states + time_step * ((forward_one - back_two) * back_one - states + forcing)
    slab_cells = planes_dev * plane_cells
    local_cells = obs_cell - space_index * slab_cells
    observed = jnp.take(states.reshape(members_dev, slab_cells), local_cells, axis=1)
    own_planes = obs_cell // plane_cells
    own_rows = lax.all_gather(observed, "mem", axis=0, tiled=True)
    own_mean = jnp.sum(own_rows, axis=0) / members
    own_anom = own_rows - own_mean
    stacked = jnp.concatenate([own_anom, own_planes.astype(jnp.float32)[None, :]], axis=0)
    band = collect_band(stacked, 1, reach_slabs, move_obs)
    context_anom = band[:members]
    context_planes = band[members].astype(jnp.int32)
    context_count = context_anom.shape[1]
    taper_block = taper_of(own_planes, context_planes, planes_all, reach_planes)
    gram_block = jnp.dot(own_anom.T, context_anom, precision=highest) / (members - 1)
    diagonal = jnp.arange(context_count)[None, :] == (band_width + jnp.arange(obs_dev))[:, None]
    covariance = taper_block * gram_block + jnp.where(diagonal, obs_var[:, None], 0.0)
    row_max = jnp.max(jnp.sum(jnp.abs(covariance), axis=1))
    var_min = jnp.min(obs_var)
    both = lax.pmax((row_max, -var_min), "space")
    upper_bound = both[0]
    lower_bound = -both[1]
    mean_rhs = obs_value - own_mean
    member_anom = lax.dynamic_slice_in_dim(own_anom, mem_index * members_dev, members_dev, 0)
    anom_rhs = (jnp.sqrt(obs_var)[None, :] * obs_noise - member_anom).T
    center = (upper_bound + lower_bound) / 2.0
    radius = (upper_bound - lower_bound) / 2.0
    sigma_ratio = center / radius
    rho_now = 1.0 / sigma_ratio
    resid_anom, resid_mean = (anom_rhs, mean_rhs)
    dir_anom, dir_mean = (anom_rhs / center, mean_rhs / center)
    anom_weight = jnp.zeros_like(anom_rhs)
    mean_weight = jnp.zeros_like(mean_rhs)
    for iteration in range(ITERS):
        anom_weight = anom_weight + dir_anom
        mean_weight = mean_weight + dir_mean
        if iteration < ITERS - 1:
            joined = jnp.concatenate([dir_anom, dir_mean[:, None]], axis=1)
            band_dirs = collect_band(joined, 0, reach_slabs, move_directions)
            image = jnp.dot(covariance, band_dirs, precision=highest)
            image_anom = image[:, :-1]
            image_mean = image[:, -1]
            resid_anom = resid_anom - image_anom
            resid_mean = resid_mean - image_mean
            rho_next = 1.0 / (2.0 * sigma_ratio - rho_now)
            dir_anom = rho_next * rho_now * dir_anom + 2.0 * rho_next / radius * resid_anom
            dir_mean = rho_next * rho_now * dir_mean + 2.0 * rho_next / radius * resid_mean
            rho_now = rho_next
    weight = anom_weight + mean_weight[:, None]
    owned_cells = lax.all_to_all(states, "mem", split_axis=2, concat_axis=0, tiled=True)
    weight_rows = lax.all_gather(weight, "mem", axis=1, tiled=True)
    weight_context = collect_band(weight_rows, 0, reach_slabs, move_weights)
    own_plane_ids = space_index * planes_dev + jnp.arange(planes_dev, dtype=jnp.int32)
    plane_taper = taper_of(own_plane_ids, context_planes, planes_all, reach_planes)

    def plane_gain(taper_row):
        return jnp.dot(context_anom * taper_row[None, :], weight_context, precision=highest)

    gain_blocks = lax.map(plane_gain, plane_taper)
    state_mean = jnp.sum(owned_cells, axis=0) / members
    state_anom = owned_cells - state_mean
    update = jnp.einsum("jxp,xjk->kxp", state_anom, gain_blocks, precision=highest) / (members - 1)
    analysis = owned_cells + update
    return lax.all_to_all(analysis, "mem", split_axis=0, concat_axis=2, tiled=True)


def solution(mesh):
    placed = (
        P("mem", "space", None),
        P("space", None),
        P("space"),
        P("space"),
        P("space"),
        P("mem", "space"),
    )
    return jax.shard_map(
        shards, mesh=mesh, in_specs=placed, out_specs=P("mem", "space", None), check_vma=False
    )
```

profile of v0, /device:TPU:6, one launch (start us, length us, event | category | flops | bytes accessed | tf_op | source)
XLA Modules:
  0.0 197.6 jit_solution(11910632786536468640)
XLA Ops:
  1.9 10.0 %collective-permute-done = f32[32,2,2048]{2,0,1:T(8,128)S(1)} collective-permute-done((f32[32,2,2048]{2,0,1:T(8,128)S(1)}, f32[32,2,2048]{2,0,1:T(8,128)S(1)}, u32[]{:S(2)}, u32[]{:S(2)}) %collective-permute-start) | collective-permute-done | bytes 524320 | tf_op jit(solution)/shard_map/ppermute | solution.py:26
  12.0 3.6 %collective-permute-done.1 = f32[32,2,2048]{2,0,1:T(8,128)S(1)} collective-permute-done((f32[32,2,2048]{2,0,1:T(8,128)S(1)}, f32[32,2,2048]{2,0,1:T(8,128)S(1)}, u32[]{:S(2)}, u32[]{:S(2)}) %collective-permute-start.1) | collective-permute-done | bytes 524320 | tf_op jit(solution)/shard_map/ppermute | solution.py:25
  16.5 1.7 collective-permute-start.2
  18.3 10.7 %collective-permute-done.3 = f32[32,2,2048]{2,0,1:T(8,128)S(1)} collective-permute-done((f32[32,2,2048]{2,0,1:T(8,128)S(1)}, f32[32,2,2048]{2,0,1:T(8,128)S(1)}, u32[]{:S(2)}, u32[]{:S(2)}) %collective-permute-start.3) | collective-permute-done | bytes 524320 | tf_op jit(solution)/shard_map/ppermute | solution.py:25
  30.0 2.2 %collective-permute-start.4 = (f32[32,2,2048]{2,0,1:T(8,128)S(1)}, f32[32,2,2048]{2,0,1:T(8,128)S(1)}, u32[]{:S(2)}, u32[]{:S(2)}) collective-permute-start(f32[32,2,2048]{2,0,1:T(8,128)S(1)} %fusion.23), channel_id=1, source_target_pairs={{1,0},{2,1},{3,2},{4,3},{5,4},{6,5},{7,6},{0,7},{9,8},{10,9},{11,1... | collective-permute-start | bytes 1572872 | tf_op jit(solution)/shard_map/ppermute | solution.py:26
  33.4 7.9 %collective-permute-done.5 = f32[32,2,2048]{2,0,1:T(8,128)S(1)} collective-permute-done((f32[32,2,2048]{2,0,1:T(8,128)S(1)}, f32[32,2,2048]{2,0,1:T(8,128)S(1)}, u32[]{:S(2)}, u32[]{:S(2)}) %collective-permute-start.5) | collective-permute-done | bytes 524320 | tf_op jit(solution)/shard_map/ppermute | solution.py:25
  41.4 2.9 %collective-permute-done.4 = f32[32,2,2048]{2,0,1:T(8,128)S(1)} collective-permute-done((f32[32,2,2048]{2,0,1:T(8,128)S(1)}, f32[32,2,2048]{2,0,1:T(8,128)S(1)}, u32[]{:S(2)}, u32[]{:S(2)}) %collective-permute-start.4) | collective-permute-done | bytes 524320 | tf_op jit(solution)/shard_map/ppermute | solution.py:26
  44.6 2.1 %collective-permute-start.6 = (f32[32,2,2048]{2,0,1:T(8,128)S(1)}, f32[32,2,2048]{2,0,1:T(8,128)S(1)}, u32[]{:S(2)}, u32[]{:S(2)}) collective-permute-start(f32[32,2,2048]{2,0,1:T(8,128)S(1)} %fusion.17), channel_id=1, source_target_pairs={{1,0},{2,1},{3,2},{4,3},{5,4},{6,5},{7,6},{0,7},{9,8},{10,9},{11,1... | collective-permute-start | bytes 1572872 | tf_op jit(solution)/shard_map/ppermute | solution.py:26
  46.8 9.0 %collective-permute-done.7 = f32[32,2,2048]{2,0,1:T(8,128)S(1)} collective-permute-done((f32[32,2,2048]{2,0,1:T(8,128)S(1)}, f32[32,2,2048]{2,0,1:T(8,128)S(1)}, u32[]{:S(2)}, u32[]{:S(2)}) %collective-permute-start.7) | collective-permute-done | bytes 524320 | tf_op jit(solution)/shard_map/ppermute | solution.py:25
  55.7 3.0 %collective-permute-done.6 = f32[32,2,2048]{2,0,1:T(8,128)S(1)} collective-permute-done((f32[32,2,2048]{2,0,1:T(8,128)S(1)}, f32[32,2,2048]{2,0,1:T(8,128)S(1)}, u32[]{:S(2)}, u32[]{:S(2)}) %collective-permute-start.6) | collective-permute-done | bytes 524320 | tf_op jit(solution)/shard_map/ppermute | solution.py:26
  60.1 13.4 %all_gather.6 = f32[128,128]{1,0:T(8,128)S(1)} all-gather(f32[32,128]{1,0:T(8,128)S(1)} %select_bitcast_fusion), channel_id=1, replica_groups=mesh['mem'=4,'space'=8] {'mem'}, dimensions={0}, use_global_device_ids=true | all-gather | bytes 81920 | tf_op jit(solution)/shard_map/all_gather | solution.py:82
  73.6 3.9 %collective-permute-start.8 = (f32[129,128]{1,0:T(8,128)S(1)}, f32[129,128]{1,0:T(8,128)S(1)}, u32[]{:S(2)}, u32[]{:S(2)}) collective-permute-start(f32[129,128]{1,0:T(8,128)S(1)} %pad_maximum_fusion.8), channel_id=1, source_target_pairs={{0,2},{1,3},{2,4},{3,5},{4,6},{5,7},{6,0},{7,1},{8,10},{9,11},{10,... | collective-permute-start | bytes 198152 | tf_op jit(solution)/shard_map/ppermute | solution.py:15
  79.4 2.5 %collective-permute-done.9 = f32[129,128]{1,0:T(8,128)S(1)} collective-permute-done((f32[129,128]{1,0:T(8,128)S(1)}, f32[129,128]{1,0:T(8,128)S(1)}, u32[]{:S(2)}, u32[]{:S(2)}) %collective-permute-start.9) | collective-permute-done | bytes 66080 | tf_op jit(solution)/shard_map/ppermute | solution.py:15
  84.6 11.5 %all-reduce = (f32[]{:T(128)}, f32[]{:T(128)}) all-reduce(f32[]{:T(128)} %reduce_max.9, f32[]{:T(128)S(6)} %neg.6), channel_id=1, replica_groups=mesh['mem'=4,'space'=8] {'space'}, use_global_device_ids=true, to_apply=%region_3.4 | all-reduce | flops 2 | bytes 16 | tf_op jit(solution)/shard_map/pmax | solution.py:96
  97.4 4.1 %collective-permute-start.12 = (f32[128,33]{0,1:T(8,128)S(1)}, f32[128,33]{0,1:T(8,128)S(1)}, u32[]{:S(2)}, u32[]{:S(2)}) collective-permute-start(f32[128,33]{0,1:T(8,128)S(1)} %pad_maximum_fusion.9), channel_id=1, source_target_pairs={{0,2},{1,3},{2,4},{3,5},{4,6},{5,7},{6,0},{7,1},{8,10},{9,11},{10,... | collective-permute-start | bytes 50696 | tf_op jit(solution)/shard_map/ppermute | solution.py:15
  102.9 2.8 %collective-permute-done.13 = f32[128,33]{0,1:T(8,128)S(1)} collective-permute-done((f32[128,33]{0,1:T(8,128)S(1)}, f32[128,33]{0,1:T(8,128)S(1)}, u32[]{:S(2)}, u32[]{:S(2)}) %collective-permute-start.13) | collective-permute-done | bytes 16928 | tf_op jit(solution)/shard_map/ppermute | solution.py:15
  107.6 2.4 %collective-permute-start.16 = (f32[128,33]{0,1:T(8,128)S(1)}, f32[128,33]{0,1:T(8,128)S(1)}, u32[]{:S(2)}, u32[]{:S(2)}) collective-permute-start(f32[128,33]{0,1:T(8,128)S(1)} %pad_maximum_fusion.10), channel_id=1, source_target_pairs={{0,2},{1,3},{2,4},{3,5},{4,6},{5,7},{6,0},{7,1},{8,10},{9,11},{10,... | collective-permute-start | bytes 50696 | tf_op jit(solution)/shard_map/ppermute | solution.py:15
  111.5 2.1 %collective-permute-done.17 = f32[128,33]{0,1:T(8,128)S(1)} collective-permute-done((f32[128,33]{0,1:T(8,128)S(1)}, f32[128,33]{0,1:T(8,128)S(1)}, u32[]{:S(2)}, u32[]{:S(2)}) %collective-permute-start.17) | collective-permute-done | bytes 16928 | tf_op jit(solution)/shard_map/ppermute | solution.py:15
  115.4 2.4 %collective-permute-start.20 = (f32[128,33]{0,1:T(8,128)S(1)}, f32[128,33]{0,1:T(8,128)S(1)}, u32[]{:S(2)}, u32[]{:S(2)}) collective-permute-start(f32[128,33]{0,1:T(8,128)S(1)} %pad_maximum_fusion.11), channel_id=1, source_target_pairs={{0,2},{1,3},{2,4},{3,5},{4,6},{5,7},{6,0},{7,1},{8,10},{9,11},{10,... | collective-permute-start | bytes 50696 | tf_op jit(solution)/shard_map/ppermute | solution.py:15
  119.3 2.1 %collective-permute-done.21 = f32[128,33]{0,1:T(8,128)S(1)} collective-permute-done((f32[128,33]{0,1:T(8,128)S(1)}, f32[128,33]{0,1:T(8,128)S(1)}, u32[]{:S(2)}, u32[]{:S(2)}) %collective-permute-start.21) | collective-permute-done | bytes 16928 | tf_op jit(solution)/shard_map/ppermute | solution.py:15
  123.3 2.4 %collective-permute-start.24 = (f32[128,33]{0,1:T(8,128)S(1)}, f32[128,33]{0,1:T(8,128)S(1)}, u32[]{:S(2)}, u32[]{:S(2)}) collective-permute-start(f32[128,33]{0,1:T(8,128)S(1)} %pad_maximum_fusion.12), channel_id=1, source_target_pairs={{0,2},{1,3},{2,4},{3,5},{4,6},{5,7},{6,0},{7,1},{8,10},{9,11},{10,... | collective-permute-start | bytes 50696 | tf_op jit(solution)/shard_map/ppermute | solution.py:15
  127.2 2.1 %collective-permute-done.25 = f32[128,33]{0,1:T(8,128)S(1)} collective-permute-done((f32[128,33]{0,1:T(8,128)S(1)}, f32[128,33]{0,1:T(8,128)S(1)}, u32[]{:S(2)}, u32[]{:S(2)}) %collective-permute-start.25) | collective-permute-done | bytes 16928 | tf_op jit(solution)/shard_map/ppermute | solution.py:15
  131.1 2.4 %collective-permute-start.28 = (f32[128,33]{0,1:T(8,128)S(1)}, f32[128,33]{0,1:T(8,128)S(1)}, u32[]{:S(2)}, u32[]{:S(2)}) collective-permute-start(f32[128,33]{0,1:T(8,128)S(1)} %pad_maximum_fusion.13), channel_id=1, source_target_pairs={{0,2},{1,3},{2,4},{3,5},{4,6},{5,7},{6,0},{7,1},{8,10},{9,11},{10,... | collective-permute-start | bytes 50696 | tf_op jit(solution)/shard_map/ppermute | solution.py:15
  134.6 2.9 %reshape.39 = f32[4,1,32768]{2,1,0:T(1,128)} reshape(f32[2048,2,32]{2,1,0:T(2,128)S(1)} %bitcast.106) | data formatting | bytes 1048576
  137.5 4.7 %all-to-all-start = ((f32[4,1,32768]{2,1,0:T(1,128)}), f32[4,1,32768]{2,1,0:T(1,128)S(1)}, u32[]{:S(2)}, u32[]{:S(2)}) async-start(f32[4,1,32768]{2,1,0:T(1,128)} %reshape.39), calls=%async_computation | async-start | bytes 1048576 | tf_op jit(solution)/shard_map/all_to_all | solution.py:126
  142.8 2.9 %collective-permute-done.29 = f32[128,33]{0,1:T(8,128)S(1)} collective-permute-done((f32[128,33]{0,1:T(8,128)S(1)}, f32[128,33]{0,1:T(8,128)S(1)}, u32[]{:S(2)}, u32[]{:S(2)}) %collective-permute-start.29) | collective-permute-done | bytes 16928 | tf_op jit(solution)/shard_map/ppermute | solution.py:15
  147.5 13.8 %all_gather.7 = f32[128,128]{0,1:T(8,128)S(1)} all-gather(f32[128,32]{0,1:T(8,128)S(1)} %fusion.38), channel_id=1, replica_groups=mesh['mem'=4,'space'=8] {'mem'}, dimensions={1}, use_global_device_ids=true | all-gather | bytes 81920 | tf_op jit(solution)/shard_map/all_gather | solution.py:127
  161.3 2.3 %collective-permute-start.32 = (f32[128,128]{0,1:T(8,128)S(1)}, f32[128,128]{0,1:T(8,128)S(1)}, u32[]{:S(2)}, u32[]{:S(2)}) collective-permute-start(f32[128,128]{0,1:T(8,128)S(1)} %all_gather.7), channel_id=1, source_target_pairs={{0,2},{1,3},{2,4},{3,5},{4,6},{5,7},{6,0},{7,1},{8,10},{9,11},{10,... | collective-permute-start | bytes 196616 | tf_op jit(solution)/shard_map/ppermute | solution.py:15
  165.6 2.8 %collective-permute-done.33 = f32[128,128]{0,1:T(8,128)S(1)} collective-permute-done((f32[128,128]{0,1:T(8,128)S(1)}, f32[128,128]{0,1:T(8,128)S(1)}, u32[]{:S(2)}, u32[]{:S(2)}) %collective-permute-start.33) | collective-permute-done | bytes 65568 | tf_op jit(solution)/shard_map/ppermute | solution.py:15
  171.2 2.1 %reduce.5 = f32[4,32768]{1,0:T(4,128)S(1)} reduce(f32[4,1,32768]{2,1,0:T(1,128)S(1)} %all-to-all-done, f32[]{:T(128)} %broadcast.56), dimensions={1}, to_apply=%all_to_all.26.reduce_sub_computation | reduce | bytes 1048580 | tf_op jit(solution)/shard_map/all_to_all | solution.py:126
  173.3 1.8 reshape.40
  177.2 19.5 %all_to_all.36 = f32[128,2,512]{2,1,0:T(2,128)S(1)} all-to-all(f32[128,2,512]{2,1,0:T(2,128)S(1)} %copy.43), channel_id=1, replica_groups=mesh['mem'=4,'space'=8] {'mem'}, dimensions={0} | all-to-all | bytes 1048576 | tf_op jit(solution)/shard_map/all_to_all | solution.py:140
  (158 shorter events, 34.7 us)
Async XLA Ops:
  1.4 10.6 %collective-permute-start = (f32[32,2,2048]{2,0,1:T(8,128)S(1)}, f32[32,2,2048]{2,0,1:T(8,128)S(1)}, u32[]{:S(2)}, u32[]{:S(2)}) collective-permute-start(f32[32,2,2048]{2,0,1:T(8,128)S(1)} %copy.36), channel_id=1, source_target_pairs={{1,0},{2,1},{3,2},{4,3},{5,4},{6,5},{7,6},{0,7},{9,8},{10,9},{11,1... | collective-permute-start | bytes 1572872 | tf_op jit(solution)/shard_map/ppermute | solution.py:26
  1.4 14.2 %collective-permute-start.1 = (f32[32,2,2048]{2,0,1:T(8,128)S(1)}, f32[32,2,2048]{2,0,1:T(8,128)S(1)}, u32[]{:S(2)}, u32[]{:S(2)}) collective-permute-start(f32[32,2,2048]{2,0,1:T(8,128)S(1)} %copy.36), channel_id=1, source_target_pairs={{0,1},{1,2},{2,3},{3,4},{4,5},{5,6},{6,7},{7,0},{8,9},{9,10},{10,1... | collective-permute-start | bytes 1572872 | tf_op jit(solution)/shard_map/ppermute | solution.py:25
  16.5 12.5 %collective-permute-start.3 = (f32[32,2,2048]{2,0,1:T(8,128)S(1)}, f32[32,2,2048]{2,0,1:T(8,128)S(1)}, u32[]{:S(2)}, u32[]{:S(2)}) collective-permute-start(f32[32,2,2048]{2,0,1:T(8,128)S(1)} %fusion.29), channel_id=1, source_target_pairs={{0,1},{1,2},{2,3},{3,4},{4,5},{5,6},{6,7},{7,0},{8,9},{9,10},{10,1... | collective-permute-start | bytes 1572872 | tf_op jit(solution)/shard_map/ppermute | solution.py:25
  16.5 13.3 %collective-permute-start.2 = (f32[32,2,2048]{2,0,1:T(8,128)S(1)}, f32[32,2,2048]{2,0,1:T(8,128)S(1)}, u32[]{:S(2)}, u32[]{:S(2)}) collective-permute-start(f32[32,2,2048]{2,0,1:T(8,128)S(1)} %fusion.29), channel_id=1, source_target_pairs={{1,0},{2,1},{3,2},{4,3},{5,4},{6,5},{7,6},{0,7},{9,8},{10,9},{11,1... | collective-permute-start | bytes 1572872 | tf_op jit(solution)/shard_map/ppermute | solution.py:26
  29.9 11.5 %collective-permute-start.5 = (f32[32,2,2048]{2,0,1:T(8,128)S(1)}, f32[32,2,2048]{2,0,1:T(8,128)S(1)}, u32[]{:S(2)}, u32[]{:S(2)}) collective-permute-start(f32[32,2,2048]{2,0,1:T(8,128)S(1)} %fusion.23), channel_id=1, source_target_pairs={{0,1},{1,2},{2,3},{3,4},{4,5},{5,6},{6,7},{7,0},{8,9},{9,10},{10,1... | collective-permute-start | bytes 1572872 | tf_op jit(solution)/shard_map/ppermute | solution.py:25
  30.0 14.3 %collective-permute-start.4 = (f32[32,2,2048]{2,0,1:T(8,128)S(1)}, f32[32,2,2048]{2,0,1:T(8,128)S(1)}, u32[]{:S(2)}, u32[]{:S(2)}) collective-permute-start(f32[32,2,2048]{2,0,1:T(8,128)S(1)} %fusion.23), channel_id=1, source_target_pairs={{1,0},{2,1},{3,2},{4,3},{5,4},{6,5},{7,6},{0,7},{9,8},{10,9},{11,1... | collective-permute-start | bytes 1572872 | tf_op jit(solution)/shard_map/ppermute | solution.py:26
  44.4 11.3 %collective-permute-start.7 = (f32[32,2,2048]{2,0,1:T(8,128)S(1)}, f32[32,2,2048]{2,0,1:T(8,128)S(1)}, u32[]{:S(2)}, u32[]{:S(2)}) collective-permute-start(f32[32,2,2048]{2,0,1:T(8,128)S(1)} %fusion.17), channel_id=1, source_target_pairs={{0,1},{1,2},{2,3},{3,4},{4,5},{5,6},{6,7},{7,0},{8,9},{9,10},{10,1... | collective-permute-start | bytes 1572872 | tf_op jit(solution)/shard_map/ppermute | solution.py:25
  44.6 14.1 %collective-permute-start.6 = (f32[32,2,2048]{2,0,1:T(8,128)S(1)}, f32[32,2,2048]{2,0,1:T(8,128)S(1)}, u32[]{:S(2)}, u32[]{:S(2)}) collective-permute-start(f32[32,2,2048]{2,0,1:T(8,128)S(1)} %fusion.17), channel_id=1, source_target_pairs={{1,0},{2,1},{3,2},{4,3},{5,4},{6,5},{7,6},{0,7},{9,8},{10,9},{11,1... | collective-permute-start | bytes 1572872 | tf_op jit(solution)/shard_map/ppermute | solution.py:26
  73.6 5.9 %collective-permute-start.8 = (f32[129,128]{1,0:T(8,128)S(1)}, f32[129,128]{1,0:T(8,128)S(1)}, u32[]{:S(2)}, u32[]{:S(2)}) collective-permute-start(f32[129,128]{1,0:T(8,128)S(1)} %pad_maximum_fusion.8), channel_id=1, source_target_pairs={{0,2},{1,3},{2,4},{3,5},{4,6},{5,7},{6,0},{7,1},{8,10},{9,11},{10,... | collective-permute-start | bytes 198152 | tf_op jit(solution)/shard_map/ppermute | solution.py:15
  77.5 5.8 %collective-permute-start.11 = (f32[129,128]{1,0:T(8,128)S(1)}, f32[129,128]{1,0:T(8,128)S(1)}, u32[]{:S(2)}, u32[]{:S(2)}) collective-permute-start(f32[129,128]{1,0:T(8,128)S(1)} %pad_maximum_fusion.8), channel_id=1, source_target_pairs={{0,6},{1,7},{2,0},{3,1},{4,2},{5,3},{6,4},{7,5},{8,14},{9,15},{10,... | collective-permute-start | bytes 198152 | tf_op jit(solution)/shard_map/ppermute | solution.py:15
  77.5 4.4 %collective-permute-start.10 = (f32[129,128]{1,0:T(8,128)S(1)}, f32[129,128]{1,0:T(8,128)S(1)}, u32[]{:S(2)}, u32[]{:S(2)}) collective-permute-start(f32[129,128]{1,0:T(8,128)S(1)} %pad_maximum_fusion.8), channel_id=1, source_target_pairs={{0,7},{1,0},{2,1},{3,2},{4,3},{5,4},{6,5},{7,6},{8,15},{9,8},{10,9... | collective-permute-start | bytes 198152 | tf_op jit(solution)/shard_map/ppermute | solution.py:15
  77.5 4.4 %collective-permute-start.9 = (f32[129,128]{1,0:T(8,128)S(1)}, f32[129,128]{1,0:T(8,128)S(1)}, u32[]{:S(2)}, u32[]{:S(2)}) collective-permute-start(f32[129,128]{1,0:T(8,128)S(1)} %pad_maximum_fusion.8), channel_id=1, source_target_pairs={{0,1},{1,2},{2,3},{3,4},{4,5},{5,6},{6,7},{7,0},{8,9},{9,10},{10,1... | collective-permute-start | bytes 198152 | tf_op jit(solution)/shard_map/ppermute | solution.py:15
  97.4 5.6 %collective-permute-start.12 = (f32[128,33]{0,1:T(8,128)S(1)}, f32[128,33]{0,1:T(8,128)S(1)}, u32[]{:S(2)}, u32[]{:S(2)}) collective-permute-start(f32[128,33]{0,1:T(8,128)S(1)} %pad_maximum_fusion.9), channel_id=1, source_target_pairs={{0,2},{1,3},{2,4},{3,5},{4,6},{5,7},{6,0},{7,1},{8,10},{9,11},{10,... | collective-permute-start | bytes 50696 | tf_op jit(solution)/shard_map/ppermute | solution.py:15
  102.2 4.8 %collective-permute-start.15 = (f32[128,33]{0,1:T(8,128)S(1)}, f32[128,33]{0,1:T(8,128)S(1)}, u32[]{:S(2)}, u32[]{:S(2)}) collective-permute-start(f32[128,33]{0,1:T(8,128)S(1)} %pad_maximum_fusion.9), channel_id=1, source_target_pairs={{0,6},{1,7},{2,0},{3,1},{4,2},{5,3},{6,4},{7,5},{8,14},{9,15},{10,... | collective-permute-start | bytes 50696 | tf_op jit(solution)/shard_map/ppermute | solution.py:15
  102.3 3.5 %collective-permute-start.14 = (f32[128,33]{0,1:T(8,128)S(1)}, f32[128,33]{0,1:T(8,128)S(1)}, u32[]{:S(2)}, u32[]{:S(2)}) collective-permute-start(f32[128,33]{0,1:T(8,128)S(1)} %pad_maximum_fusion.9), channel_id=1, source_target_pairs={{0,7},{1,0},{2,1},{3,2},{4,3},{5,4},{6,5},{7,6},{8,15},{9,8},{10,9... | collective-permute-start | bytes 50696 | tf_op jit(solution)/shard_map/ppermute | solution.py:15
  107.6 3.9 %collective-permute-start.16 = (f32[128,33]{0,1:T(8,128)S(1)}, f32[128,33]{0,1:T(8,128)S(1)}, u32[]{:S(2)}, u32[]{:S(2)}) collective-permute-start(f32[128,33]{0,1:T(8,128)S(1)} %pad_maximum_fusion.10), channel_id=1, source_target_pairs={{0,2},{1,3},{2,4},{3,5},{4,6},{5,7},{6,0},{7,1},{8,10},{9,11},{10,... | collective-permute-start | bytes 50696 | tf_op jit(solution)/shard_map/ppermute | solution.py:15
  110.1 4.8 %collective-permute-start.19 = (f32[128,33]{0,1:T(8,128)S(1)}, f32[128,33]{0,1:T(8,128)S(1)}, u32[]{:S(2)}, u32[]{:S(2)}) collective-permute-start(f32[128,33]{0,1:T(8,128)S(1)} %pad_maximum_fusion.10), channel_id=1, source_target_pairs={{0,6},{1,7},{2,0},{3,1},{4,2},{5,3},{6,4},{7,5},{8,14},{9,15},{10,... | collective-permute-start | bytes 50696 | tf_op jit(solution)/shard_map/ppermute | solution.py:15
  110.1 3.5 %collective-permute-start.18 = (f32[128,33]{0,1:T(8,128)S(1)}, f32[128,33]{0,1:T(8,128)S(1)}, u32[]{:S(2)}, u32[]{:S(2)}) collective-permute-start(f32[128,33]{0,1:T(8,128)S(1)} %pad_maximum_fusion.10), channel_id=1, source_target_pairs={{0,7},{1,0},{2,1},{3,2},{4,3},{5,4},{6,5},{7,6},{8,15},{9,8},{10,9... | collective-permute-start | bytes 50696 | tf_op jit(solution)/shard_map/ppermute | solution.py:15
  115.4 3.9 %collective-permute-start.20 = (f32[128,33]{0,1:T(8,128)S(1)}, f32[128,33]{0,1:T(8,128)S(1)}, u32[]{:S(2)}, u32[]{:S(2)}) collective-permute-start(f32[128,33]{0,1:T(8,128)S(1)} %pad_maximum_fusion.11), channel_id=1, source_target_pairs={{0,2},{1,3},{2,4},{3,5},{4,6},{5,7},{6,0},{7,1},{8,10},{9,11},{10,... | collective-permute-start | bytes 50696 | tf_op jit(solution)/shard_map/ppermute | solution.py:15
  117.9 4.8 %collective-permute-start.23 = (f32[128,33]{0,1:T(8,128)S(1)}, f32[128,33]{0,1:T(8,128)S(1)}, u32[]{:S(2)}, u32[]{:S(2)}) collective-permute-start(f32[128,33]{0,1:T(8,128)S(1)} %pad_maximum_fusion.11), channel_id=1, source_target_pairs={{0,6},{1,7},{2,0},{3,1},{4,2},{5,3},{6,4},{7,5},{8,14},{9,15},{10,... | collective-permute-start | bytes 50696 | tf_op jit(solution)/shard_map/ppermute | solution.py:15
  118.0 3.5 %collective-permute-start.22 = (f32[128,33]{0,1:T(8,128)S(1)}, f32[128,33]{0,1:T(8,128)S(1)}, u32[]{:S(2)}, u32[]{:S(2)}) collective-permute-start(f32[128,33]{0,1:T(8,128)S(1)} %pad_maximum_fusion.11), channel_id=1, source_target_pairs={{0,7},{1,0},{2,1},{3,2},{4,3},{5,4},{6,5},{7,6},{8,15},{9,8},{10,9... | collective-permute-start | bytes 50696 | tf_op jit(solution)/shard_map/ppermute | solution.py:15
  123.3 3.9 %collective-permute-start.24 = (f32[128,33]{0,1:T(8,128)S(1)}, f32[128,33]{0,1:T(8,128)S(1)}, u32[]{:S(2)}, u32[]{:S(2)}) collective-permute-start(f32[128,33]{0,1:T(8,128)S(1)} %pad_maximum_fusion.12), channel_id=1, source_target_pairs={{0,2},{1,3},{2,4},{3,5},{4,6},{5,7},{6,0},{7,1},{8,10},{9,11},{10,... | collective-permute-start | bytes 50696 | tf_op jit(solution)/shard_map/ppermute | solution.py:15
  125.8 4.8 %collective-permute-start.27 = (f32[128,33]{0,1:T(8,128)S(1)}, f32[128,33]{0,1:T(8,128)S(1)}, u32[]{:S(2)}, u32[]{:S(2)}) collective-permute-start(f32[128,33]{0,1:T(8,128)S(1)} %pad_maximum_fusion.12), channel_id=1, source_target_pairs={{0,6},{1,7},{2,0},{3,1},{4,2},{5,3},{6,4},{7,5},{8,14},{9,15},{10,... | collective-permute-start | bytes 50696 | tf_op jit(solution)/shard_map/ppermute | solution.py:15
  125.8 3.5 %collective-permute-start.26 = (f32[128,33]{0,1:T(8,128)S(1)}, f32[128,33]{0,1:T(8,128)S(1)}, u32[]{:S(2)}, u32[]{:S(2)}) collective-permute-start(f32[128,33]{0,1:T(8,128)S(1)} %pad_maximum_fusion.12), channel_id=1, source_target_pairs={{0,7},{1,0},{2,1},{3,2},{4,3},{5,4},{6,5},{7,6},{8,15},{9,8},{10,9... | collective-permute-start | bytes 50696 | tf_op jit(solution)/shard_map/ppermute | solution.py:15
  131.1 11.7 %collective-permute-start.28 = (f32[128,33]{0,1:T(8,128)S(1)}, f32[128,33]{0,1:T(8,128)S(1)}, u32[]{:S(2)}, u32[]{:S(2)}) collective-permute-start(f32[128,33]{0,1:T(8,128)S(1)} %pad_maximum_fusion.13), channel_id=1, source_target_pairs={{0,2},{1,3},{2,4},{3,5},{4,6},{5,7},{6,0},{7,1},{8,10},{9,11},{10,... | collective-permute-start | bytes 50696 | tf_op jit(solution)/shard_map/ppermute | solution.py:15
  137.5 33.2 %all-to-all-start = ((f32[4,1,32768]{2,1,0:T(1,128)}), f32[4,1,32768]{2,1,0:T(1,128)S(1)}, u32[]{:S(2)}, u32[]{:S(2)}) async-start(f32[4,1,32768]{2,1,0:T(1,128)} %reshape.39), calls=%async_computation | async-start | bytes 1048576 | tf_op jit(solution)/shard_map/all_to_all | solution.py:126
  142.2 4.8 %collective-permute-start.31 = (f32[128,33]{0,1:T(8,128)S(1)}, f32[128,33]{0,1:T(8,128)S(1)}, u32[]{:S(2)}, u32[]{:S(2)}) collective-permute-start(f32[128,33]{0,1:T(8,128)S(1)} %pad_maximum_fusion.13), channel_id=1, source_target_pairs={{0,6},{1,7},{2,0},{3,1},{4,2},{5,3},{6,4},{7,5},{8,14},{9,15},{10,... | collective-permute-start | bytes 50696 | tf_op jit(solution)/shard_map/ppermute | solution.py:15
  142.3 3.5 %collective-permute-start.30 = (f32[128,33]{0,1:T(8,128)S(1)}, f32[128,33]{0,1:T(8,128)S(1)}, u32[]{:S(2)}, u32[]{:S(2)}) collective-permute-start(f32[128,33]{0,1:T(8,128)S(1)} %pad_maximum_fusion.13), channel_id=1, source_target_pairs={{0,7},{1,0},{2,1},{3,2},{4,3},{5,4},{6,5},{7,6},{8,15},{9,8},{10,9... | collective-permute-start | bytes 50696 | tf_op jit(solution)/shard_map/ppermute | solution.py:15
  161.3 4.3 %collective-permute-start.32 = (f32[128,128]{0,1:T(8,128)S(1)}, f32[128,128]{0,1:T(8,128)S(1)}, u32[]{:S(2)}, u32[]{:S(2)}) collective-permute-start(f32[128,128]{0,1:T(8,128)S(1)} %all_gather.7), channel_id=1, source_target_pairs={{0,2},{1,3},{2,4},{3,5},{4,6},{5,7},{6,0},{7,1},{8,10},{9,11},{10,... | collective-permute-start | bytes 196616 | tf_op jit(solution)/shard_map/ppermute | solution.py:15
  163.7 5.7 %collective-permute-start.35 = (f32[128,128]{0,1:T(8,128)S(1)}, f32[128,128]{0,1:T(8,128)S(1)}, u32[]{:S(2)}, u32[]{:S(2)}) collective-permute-start(f32[128,128]{0,1:T(8,128)S(1)} %all_gather.7), channel_id=1, source_target_pairs={{0,6},{1,7},{2,0},{3,1},{4,2},{5,3},{6,4},{7,5},{8,14},{9,15},{10,... | collective-permute-start | bytes 196616 | tf_op jit(solution)/shard_map/ppermute | solution.py:15
  163.8 4.7 %collective-permute-start.34 = (f32[128,128]{0,1:T(8,128)S(1)}, f32[128,128]{0,1:T(8,128)S(1)}, u32[]{:S(2)}, u32[]{:S(2)}) collective-permute-start(f32[128,128]{0,1:T(8,128)S(1)} %all_gather.7), channel_id=1, source_target_pairs={{0,7},{1,0},{2,1},{3,2},{4,3},{5,4},{6,5},{7,6},{8,15},{9,8},{10,9... | collective-permute-start | bytes 196616 | tf_op jit(solution)/shard_map/ppermute | solution.py:15
  163.8 4.6 %collective-permute-start.33 = (f32[128,128]{0,1:T(8,128)S(1)}, f32[128,128]{0,1:T(8,128)S(1)}, u32[]{:S(2)}, u32[]{:S(2)}) collective-permute-start(f32[128,128]{0,1:T(8,128)S(1)} %all_gather.7), channel_id=1, source_target_pairs={{0,1},{1,2},{2,3},{3,4},{4,5},{5,6},{6,7},{7,0},{8,9},{9,10},{10,1... | collective-permute-start | bytes 196616 | tf_op jit(solution)/shard_map/ppermute | solution.py:15
  (11 other events, 216.9 us)
where the time goes:
time: 198 us
  waiting for transfers between devices  78.8 us (40%)
  blocking collectives  58.2 us (29%)
  starting transfers between devices  35.7 us (18%)
  local copies, waits for them, and re-layouts  11.4 us (6%)
  other arithmetic  5.05 us (3%)
  matrix products  4.71 us (2%)
  between operations  3.71 us (2%)
    ppermute x4, waiting for transfers between devices, padded_2(): before = lax.ppermute(last, axis, up)  31.3 us
    ppermute x28, waiting for transfers between devices, from_behind(): return lax.ppermute(value, axis, pairs)  30.8 us
    ppermute x28, starting transfers between devices, from_behind(): return lax.ppermute(value, axis, pairs)  24.1 us
    all_to_all x1, blocking collectives, shards(): lax.all_to_all(analysis, 'mem', split_axis=0, concat_axis=2, tiled=True)  19.5 us
    ppermute x4, waiting for transfers between devices, padded_2(): after = lax.ppermute(initial, axis, down)  16.7 us
    all_gather x1, blocking collectives, shards(): weight_rows = lax.all_gather(weight, 'mem', axis=1, tiled=True)  13.8 us
    all_gather x1, blocking collectives, shards(): own_rows = lax.all_gather(observed, 'mem', axis=0, tiled=True)  13.4 us
    pmax x1, blocking collectives, shards(): both = lax.pmax((row_max, -var_min), 'space')  11.5 us
  transfers between devices with their start and end apart: 37, of which 27 were waited for; matrix products, arithmetic and copies ran while one was open for 3% of the time, Pallas kernels for 0%

commit v1 on v0

--- a/solution.py
+++ b/solution.py
@@ -7,6 +7,24 @@
 ITERS = 6
 time_step = 0.05
 highest = lax.Precision.HIGHEST
+
+
+def laid_out(blocks, dim):
+    lengths = list(blocks.shape[1:])
+    lengths[dim] *= blocks.shape[0]
+    return jnp.moveaxis(blocks, 0, dim).reshape(lengths)
+
+
+def grow_blocks(array, axis):
+    peers = lax.axis_size(axis)
+    parts = array[None]
+    for level in range(peers.bit_length() - 1):
+        stride = 1 << level
+        other = lax.ppermute(parts, axis, [(i, i ^ stride) for i in range(peers)])
+        both = jnp.stack([parts, other])
+        upper = lax.axis_index(axis) >> level & 1
+        parts = jnp.where(upper == 0, both, both[::-1]).reshape(-1, *array.shape)
+    return parts
 
 
 def from_behind(value, axis, steps):
@@ -124,7 +142,7 @@
             rho_now = rho_next
     weight = anom_weight + mean_weight[:, None]
     owned_cells = lax.all_to_all(states, "mem", split_axis=2, concat_axis=0, tiled=True)
-    weight_rows = lax.all_gather(weight, "mem", axis=1, tiled=True)
+    weight_rows = laid_out(grow_blocks(weight, "mem"), 1)
     weight_context = collect_band(weight_rows, 0, reach_slabs, move_weights)
     own_plane_ids = space_index * planes_dev + jnp.arange(planes_dev, dtype=jnp.int32)
     plane_taper = taper_of(own_plane_ids, context_planes, planes_all, reach_planes)

time: 198 us -> 190 us (0.960)
  blocking collectives: 58.2 us -> 41.3 us
  waiting for transfers between devices: 78.8 us -> 85.3 us
  starting transfers between devices: 35.7 us -> 38.2 us
    all_gather x1 -> x0, blocking collectives: 13.8 us -> none  [shards(): weight_rows = lax.all_gather(weight, 'mem', axis=1, tiled=True)]
    all_to_all x1, waiting for transfers between devices: 0.01 us -> 4.2 us  [shards(): lax.all_to_all(states, 'mem', split_axis=2, concat_axis=0, tiled=True)]
    ppermute x0 -> x2, starting transfers between devices: none -> 3.38 us  [grow_blocks(): other = lax.ppermute(parts, axis, [(i, i ^ stride) for i in range(peers)])]
    all_to_all x1, blocking collectives: 19.5 us -> 16.4 us  [shards(): lax.all_to_all(analysis, 'mem', split_axis=0, concat_axis=2, tiled=True)]
    ppermute x0 -> x2, waiting for transfers between devices: none -> 2.3 us  [grow_blocks(): other = lax.ppermute(parts, axis, [(i, i ^ stride) for i in range(peers)])]
    unnamed x37 -> x35, local copies, waits for them, and re-layouts: 6.2 us -> 6.2 us
  transfers between devices with their start and end apart: 37 -> 39, of which waited for: 27 -> 30; matrix products, arithmetic and copies ran while one was open for 3% -> 3% of each run, Pallas kernels for 0% -> 0%
where the time goes in v1:
time: 190 us
  waiting for transfers between devices  85.3 us (45%)
  blocking collectives  41.3 us (22%)
  starting transfers between devices  38.2 us (20%)
  local copies, waits for them, and re-layouts  11.4 us (6%)
  other arithmetic  5.09 us (3%)
  matrix products  4.7 us (2%)
  between operations  3.78 us (2%)
    ppermute x4, waiting for transfers between devices, padded_2(): before = lax.ppermute(last, axis, up)  31.3 us
    ppermute x28, waiting for transfers between devices, from_behind(): return lax.ppermute(value, axis, pairs)  30.8 us
    ppermute x28, starting transfers between devices, from_behind(): return lax.ppermute(value, axis, pairs)  24.4 us
    ppermute x4, waiting for transfers between devices, padded_2(): after = lax.ppermute(initial, axis, down)  16.7 us
    all_to_all x1, blocking collectives, shards(): lax.all_to_all(analysis, 'mem', split_axis=0, concat_axis=2, tiled=True)  16.4 us
    all_gather x1, blocking collectives, shards(): own_rows = lax.all_gather(observed, 'mem', axis=0, tiled=True)  13.4 us
    pmax x1, blocking collectives, shards(): both = lax.pmax((row_max, -var_min), 'space')  11.5 us
    unnamed x35, local copies, waits for them, and re-layouts  6.2 us
  transfers between devices with their start and end apart: 39, of which 30 were waited for; matrix products, arithmetic and copies ran while one was open for 3% of the time, Pallas kernels for 0%

profile of v1, /device:TPU:6, one launch (start us, length us, event | category | flops | bytes accessed | tf_op | source)
XLA Modules:
  0.0 189.9 jit_solution(15638196966442525447)
XLA Ops:
  1.9 10.0 %collective-permute-done = f32[32,2,2048]{2,0,1:T(8,128)S(1)} collective-permute-done((f32[32,2,2048]{2,0,1:T(8,128)S(1)}, f32[32,2,2048]{2,0,1:T(8,128)S(1)}, u32[]{:S(2)}, u32[]{:S(2)}) %collective-permute-start) | collective-permute-done | bytes 524320 | tf_op jit(solution)/shard_map/ppermute | solution.py:44
  12.0 3.6 %collective-permute-done.1 = f32[32,2,2048]{2,0,1:T(8,128)S(1)} collective-permute-done((f32[32,2,2048]{2,0,1:T(8,128)S(1)}, f32[32,2,2048]{2,0,1:T(8,128)S(1)}, u32[]{:S(2)}, u32[]{:S(2)}) %collective-permute-start.1) | collective-permute-done | bytes 524320 | tf_op jit(solution)/shard_map/ppermute | solution.py:43
  18.3 10.7 %collective-permute-done.3 = f32[32,2,2048]{2,0,1:T(8,128)S(1)} collective-permute-done((f32[32,2,2048]{2,0,1:T(8,128)S(1)}, f32[32,2,2048]{2,0,1:T(8,128)S(1)}, u32[]{:S(2)}, u32[]{:S(2)}) %collective-permute-start.3) | collective-permute-done | bytes 524320 | tf_op jit(solution)/shard_map/ppermute | solution.py:43
  30.0 2.2 %collective-permute-start.4 = (f32[32,2,2048]{2,0,1:T(8,128)S(1)}, f32[32,2,2048]{2,0,1:T(8,128)S(1)}, u32[]{:S(2)}, u32[]{:S(2)}) collective-permute-start(f32[32,2,2048]{2,0,1:T(8,128)S(1)} %fusion.23), channel_id=1, source_target_pairs={{1,0},{2,1},{3,2},{4,3},{5,4},{6,5},{7,6},{0,7},{9,8},{10,9},{11,1... | collective-permute-start | bytes 1572872 | tf_op jit(solution)/shard_map/ppermute | solution.py:44
  33.4 7.9 %collective-permute-done.5 = f32[32,2,2048]{2,0,1:T(8,128)S(1)} collective-permute-done((f32[32,2,2048]{2,0,1:T(8,128)S(1)}, f32[32,2,2048]{2,0,1:T(8,128)S(1)}, u32[]{:S(2)}, u32[]{:S(2)}) %collective-permute-start.5) | collective-permute-done | bytes 524320 | tf_op jit(solution)/shard_map/ppermute | solution.py:43
  41.4 2.9 %collective-permute-done.4 = f32[32,2,2048]{2,0,1:T(8,128)S(1)} collective-permute-done((f32[32,2,2048]{2,0,1:T(8,128)S(1)}, f32[32,2,2048]{2,0,1:T(8,128)S(1)}, u32[]{:S(2)}, u32[]{:S(2)}) %collective-permute-start.4) | collective-permute-done | bytes 524320 | tf_op jit(solution)/shard_map/ppermute | solution.py:44
  44.6 2.1 %collective-permute-start.6 = (f32[32,2,2048]{2,0,1:T(8,128)S(1)}, f32[32,2,2048]{2,0,1:T(8,128)S(1)}, u32[]{:S(2)}, u32[]{:S(2)}) collective-permute-start(f32[32,2,2048]{2,0,1:T(8,128)S(1)} %fusion.17), channel_id=1, source_target_pairs={{1,0},{2,1},{3,2},{4,3},{5,4},{6,5},{7,6},{0,7},{9,8},{10,9},{11,1... | collective-permute-start | bytes 1572872 | tf_op jit(solution)/shard_map/ppermute | solution.py:44
  46.8 9.0 %collective-permute-done.7 = f32[32,2,2048]{2,0,1:T(8,128)S(1)} collective-permute-done((f32[32,2,2048]{2,0,1:T(8,128)S(1)}, f32[32,2,2048]{2,0,1:T(8,128)S(1)}, u32[]{:S(2)}, u32[]{:S(2)}) %collective-permute-start.7) | collective-permute-done | bytes 524320 | tf_op jit(solution)/shard_map/ppermute | solution.py:43
  55.7 3.0 %collective-permute-done.6 = f32[32,2,2048]{2,0,1:T(8,128)S(1)} collective-permute-done((f32[32,2,2048]{2,0,1:T(8,128)S(1)}, f32[32,2,2048]{2,0,1:T(8,128)S(1)}, u32[]{:S(2)}, u32[]{:S(2)}) %collective-permute-start.6) | collective-permute-done | bytes 524320 | tf_op jit(solution)/shard_map/ppermute | solution.py:44
  60.1 13.4 %all_gather.3 = f32[128,128]{1,0:T(8,128)S(1)} all-gather(f32[32,128]{1,0:T(8,128)S(1)} %select_bitcast_fusion), channel_id=1, replica_groups=mesh['mem'=4,'space'=8] {'mem'}, dimensions={0}, use_global_device_ids=true | all-gather | bytes 81920 | tf_op jit(solution)/shard_map/all_gather | solution.py:100
  73.6 3.9 %collective-permute-start.8 = (f32[129,128]{1,0:T(8,128)S(1)}, f32[129,128]{1,0:T(8,128)S(1)}, u32[]{:S(2)}, u32[]{:S(2)}) collective-permute-start(f32[129,128]{1,0:T(8,128)S(1)} %pad_maximum_fusion.8), channel_id=1, source_target_pairs={{0,2},{1,3},{2,4},{3,5},{4,6},{5,7},{6,0},{7,1},{8,10},{9,11},{10,... | collective-permute-start | bytes 198152 | tf_op jit(solution)/shard_map/ppermute | solution.py:33
  79.4 2.5 %collective-permute-done.9 = f32[129,128]{1,0:T(8,128)S(1)} collective-permute-done((f32[129,128]{1,0:T(8,128)S(1)}, f32[129,128]{1,0:T(8,128)S(1)}, u32[]{:S(2)}, u32[]{:S(2)}) %collective-permute-start.9) | collective-permute-done | bytes 66080 | tf_op jit(solution)/shard_map/ppermute | solution.py:33
  84.6 11.5 %all-reduce = (f32[]{:T(128)}, f32[]{:T(128)}) all-reduce(f32[]{:T(128)} %reduce_max.9, f32[]{:T(128)S(6)} %neg.6), channel_id=1, replica_groups=mesh['mem'=4,'space'=8] {'space'}, use_global_device_ids=true, to_apply=%region_3.4 | all-reduce | flops 2 | bytes 16 | tf_op jit(solution)/shard_map/pmax | solution.py:114
  97.5 4.1 %collective-permute-start.12 = (f32[128,33]{0,1:T(8,128)S(1)}, f32[128,33]{0,1:T(8,128)S(1)}, u32[]{:S(2)}, u32[]{:S(2)}) collective-permute-start(f32[128,33]{0,1:T(8,128)S(1)} %pad_maximum_fusion.11), channel_id=1, source_target_pairs={{0,2},{1,3},{2,4},{3,5},{4,6},{5,7},{6,0},{7,1},{8,10},{9,11},{10,... | collective-permute-start | bytes 50696 | tf_op jit(solution)/shard_map/ppermute | solution.py:33
  103.0 2.8 %collective-permute-done.13 = f32[128,33]{0,1:T(8,128)S(1)} collective-permute-done((f32[128,33]{0,1:T(8,128)S(1)}, f32[128,33]{0,1:T(8,128)S(1)}, u32[]{:S(2)}, u32[]{:S(2)}) %collective-permute-start.13) | collective-permute-done | bytes 16928 | tf_op jit(solution)/shard_map/ppermute | solution.py:33
  107.7 2.4 %collective-permute-start.16 = (f32[128,33]{0,1:T(8,128)S(1)}, f32[128,33]{0,1:T(8,128)S(1)}, u32[]{:S(2)}, u32[]{:S(2)}) collective-permute-start(f32[128,33]{0,1:T(8,128)S(1)} %pad_maximum_fusion.12), channel_id=1, source_target_pairs={{0,2},{1,3},{2,4},{3,5},{4,6},{5,7},{6,0},{7,1},{8,10},{9,11},{10,... | collective-permute-start | bytes 50696 | tf_op jit(solution)/shard_map/ppermute | solution.py:33
  111.6 2.1 %collective-permute-done.17 = f32[128,33]{0,1:T(8,128)S(1)} collective-permute-done((f32[128,33]{0,1:T(8,128)S(1)}, f32[128,33]{0,1:T(8,128)S(1)}, u32[]{:S(2)}, u32[]{:S(2)}) %collective-permute-start.17) | collective-permute-done | bytes 16928 | tf_op jit(solution)/shard_map/ppermute | solution.py:33
  115.5 2.4 %collective-permute-start.20 = (f32[128,33]{0,1:T(8,128)S(1)}, f32[128,33]{0,1:T(8,128)S(1)}, u32[]{:S(2)}, u32[]{:S(2)}) collective-permute-start(f32[128,33]{0,1:T(8,128)S(1)} %pad_maximum_fusion.13), channel_id=1, source_target_pairs={{0,2},{1,3},{2,4},{3,5},{4,6},{5,7},{6,0},{7,1},{8,10},{9,11},{10,... | collective-permute-start | bytes 50696 | tf_op jit(solution)/shard_map/ppermute | solution.py:33
  119.4 2.1 %collective-permute-done.21 = f32[128,33]{0,1:T(8,128)S(1)} collective-permute-done((f32[128,33]{0,1:T(8,128)S(1)}, f32[128,33]{0,1:T(8,128)S(1)}, u32[]{:S(2)}, u32[]{:S(2)}) %collective-permute-start.21) | collective-permute-done | bytes 16928 | tf_op jit(solution)/shard_map/ppermute | solution.py:33
  123.3 2.4 %collective-permute-start.24 = (f32[128,33]{0,1:T(8,128)S(1)}, f32[128,33]{0,1:T(8,128)S(1)}, u32[]{:S(2)}, u32[]{:S(2)}) collective-permute-start(f32[128,33]{0,1:T(8,128)S(1)} %pad_maximum_fusion.14), channel_id=1, source_target_pairs={{0,2},{1,3},{2,4},{3,5},{4,6},{5,7},{6,0},{7,1},{8,10},{9,11},{10,... | collective-permute-start | bytes 50696 | tf_op jit(solution)/shard_map/ppermute | solution.py:33
  127.2 2.1 %collective-permute-done.25 = f32[128,33]{0,1:T(8,128)S(1)} collective-permute-done((f32[128,33]{0,1:T(8,128)S(1)}, f32[128,33]{0,1:T(8,128)S(1)}, u32[]{:S(2)}, u32[]{:S(2)}) %collective-permute-start.25) | collective-permute-done | bytes 16928 | tf_op jit(solution)/shard_map/ppermute | solution.py:33
  131.2 2.4 %collective-permute-start.28 = (f32[128,33]{0,1:T(8,128)S(1)}, f32[128,33]{0,1:T(8,128)S(1)}, u32[]{:S(2)}, u32[]{:S(2)}) collective-permute-start(f32[128,33]{0,1:T(8,128)S(1)} %pad_maximum_fusion.15), channel_id=1, source_target_pairs={{0,2},{1,3},{2,4},{3,5},{4,6},{5,7},{6,0},{7,1},{8,10},{9,11},{10,... | collective-permute-start | bytes 50696 | tf_op jit(solution)/shard_map/ppermute | solution.py:33
  135.1 2.1 %collective-permute-done.29 = f32[128,33]{0,1:T(8,128)S(1)} collective-permute-done((f32[128,33]{0,1:T(8,128)S(1)}, f32[128,33]{0,1:T(8,128)S(1)}, u32[]{:S(2)}, u32[]{:S(2)}) %collective-permute-start.29) | collective-permute-done | bytes 16928 | tf_op jit(solution)/shard_map/ppermute | solution.py:33
  140.5 2.3 %collective-permute-done.32 = f32[1,128,32]{1,2,0:T(8,128)S(1)} collective-permute-done((f32[1,128,32]{1,2,0:T(8,128)S(1)}, f32[1,128,32]{1,2,0:T(8,128)S(1)}, u32[]{:S(2)}, u32[]{:S(2)}) %collective-permute-start.32) | collective-permute-done | bytes 16416 | tf_op jit(solution)/shard_map/ppermute | solution.py:23
  142.8 1.9 collective-permute-start.33
  145.8 2.9 %reshape.51 = f32[4,1,32768]{2,1,0:T(1,128)} reshape(f32[2048,2,32]{2,1,0:T(2,128)S(1)} %bitcast.119) | data formatting | bytes 1048576
  148.6 3.5 %all-to-all-start = ((f32[4,1,32768]{2,1,0:T(1,128)}), f32[4,1,32768]{2,1,0:T(1,128)S(1)}, u32[]{:S(2)}, u32[]{:S(2)}) async-start(f32[4,1,32768]{2,1,0:T(1,128)} %reshape.51), calls=%async_computation | async-start | bytes 1048576 | tf_op jit(solution)/shard_map/all_to_all | solution.py:144
  152.2 2.6 %collective-permute-start.34 = (f32[128,128]{0,1:T(8,128)S(1)}, f32[128,128]{0,1:T(8,128)S(1)}, u32[]{:S(2)}, u32[]{:S(2)}) collective-permute-start(f32[128,128]{0,1:T(8,128)S(1)} %bitcast.124), channel_id=1, source_target_pairs={{0,2},{1,3},{2,4},{3,5},{4,6},{5,7},{6,0},{7,1},{8,10},{9,11},{10,... | collective-permute-start | bytes 196616 | tf_op jit(solution)/shard_map/ppermute | solution.py:33
  156.7 3.0 %collective-permute-done.35 = f32[128,128]{0,1:T(8,128)S(1)} collective-permute-done((f32[128,128]{0,1:T(8,128)S(1)}, f32[128,128]{0,1:T(8,128)S(1)}, u32[]{:S(2)}, u32[]{:S(2)}) %collective-permute-start.35) | collective-permute-done | bytes 65568 | tf_op jit(solution)/shard_map/ppermute | solution.py:33
  161.8 4.2 %all-to-all-done = f32[4,1,32768]{2,1,0:T(1,128)S(1)} async-done(((f32[4,1,32768]{2,1,0:T(1,128)}), f32[4,1,32768]{2,1,0:T(1,128)S(1)}, u32[]{:S(2)}, u32[]{:S(2)}) %all-to-all-start) | async-done | bytes 524320 | tf_op jit(solution)/shard_map/all_to_all | solution.py:144
  166.5 2.1 %reduce.5 = f32[4,32768]{1,0:T(4,128)S(1)} reduce(f32[4,1,32768]{2,1,0:T(1,128)S(1)} %all-to-all-done, f32[]{:T(128)} %broadcast.61), dimensions={1}, to_apply=%all_to_all.26.reduce_sub_computation | reduce | bytes 1048580 | tf_op jit(solution)/shard_map/all_to_all | solution.py:144
  172.5 16.4 %all_to_all.36 = f32[128,2,512]{2,1,0:T(2,128)S(1)} all-to-all(f32[128,2,512]{2,1,0:T(2,128)S(1)} %copy.49), channel_id=1, replica_groups=mesh['mem'=4,'space'=8] {'mem'}, dimensions={0} | all-to-all | bytes 1048576 | tf_op jit(solution)/shard_map/all_to_all | solution.py:158
  (163 shorter events, 40.4 us)
Async XLA Ops:
  1.4 10.6 %collective-permute-start = (f32[32,2,2048]{2,0,1:T(8,128)S(1)}, f32[32,2,2048]{2,0,1:T(8,128)S(1)}, u32[]{:S(2)}, u32[]{:S(2)}) collective-permute-start(f32[32,2,2048]{2,0,1:T(8,128)S(1)} %copy.42), channel_id=1, source_target_pairs={{1,0},{2,1},{3,2},{4,3},{5,4},{6,5},{7,6},{0,7},{9,8},{10,9},{11,1... | collective-permute-start | bytes 1572872 | tf_op jit(solution)/shard_map/ppermute | solution.py:44
  1.4 14.2 %collective-permute-start.1 = (f32[32,2,2048]{2,0,1:T(8,128)S(1)}, f32[32,2,2048]{2,0,1:T(8,128)S(1)}, u32[]{:S(2)}, u32[]{:S(2)}) collective-permute-start(f32[32,2,2048]{2,0,1:T(8,128)S(1)} %copy.42), channel_id=1, source_target_pairs={{0,1},{1,2},{2,3},{3,4},{4,5},{5,6},{6,7},{7,0},{8,9},{9,10},{10,1... | collective-permute-start | bytes 1572872 | tf_op jit(solution)/shard_map/ppermute | solution.py:43
  16.5 12.5 %collective-permute-start.3 = (f32[32,2,2048]{2,0,1:T(8,128)S(1)}, f32[32,2,2048]{2,0,1:T(8,128)S(1)}, u32[]{:S(2)}, u32[]{:S(2)}) collective-permute-start(f32[32,2,2048]{2,0,1:T(8,128)S(1)} %fusion.29), channel_id=1, source_target_pairs={{0,1},{1,2},{2,3},{3,4},{4,5},{5,6},{6,7},{7,0},{8,9},{9,10},{10,1... | collective-permute-start | bytes 1572872 | tf_op jit(solution)/shard_map/ppermute | solution.py:43
  16.5 13.3 %collective-permute-start.2 = (f32[32,2,2048]{2,0,1:T(8,128)S(1)}, f32[32,2,2048]{2,0,1:T(8,128)S(1)}, u32[]{:S(2)}, u32[]{:S(2)}) collective-permute-start(f32[32,2,2048]{2,0,1:T(8,128)S(1)} %fusion.29), channel_id=1, source_target_pairs={{1,0},{2,1},{3,2},{4,3},{5,4},{6,5},{7,6},{0,7},{9,8},{10,9},{11,1... | collective-permute-start | bytes 1572872 | tf_op jit(solution)/shard_map/ppermute | solution.py:44
  29.9 11.5 %collective-permute-start.5 = (f32[32,2,2048]{2,0,1:T(8,128)S(1)}, f32[32,2,2048]{2,0,1:T(8,128)S(1)}, u32[]{:S(2)}, u32[]{:S(2)}) collective-permute-start(f32[32,2,2048]{2,0,1:T(8,128)S(1)} %fusion.23), channel_id=1, source_target_pairs={{0,1},{1,2},{2,3},{3,4},{4,5},{5,6},{6,7},{7,0},{8,9},{9,10},{10,1... | collective-permute-start | bytes 1572872 | tf_op jit(solution)/shard_map/ppermute | solution.py:43
  30.0 14.3 %collective-permute-start.4 = (f32[32,2,2048]{2,0,1:T(8,128)S(1)}, f32[32,2,2048]{2,0,1:T(8,128)S(1)}, u32[]{:S(2)}, u32[]{:S(2)}) collective-permute-start(f32[32,2,2048]{2,0,1:T(8,128)S(1)} %fusion.23), channel_id=1, source_target_pairs={{1,0},{2,1},{3,2},{4,3},{5,4},{6,5},{7,6},{0,7},{9,8},{10,9},{11,1... | collective-permute-start | bytes 1572872 | tf_op jit(solution)/shard_map/ppermute | solution.py:44
  44.4 11.3 %collective-permute-start.7 = (f32[32,2,2048]{2,0,1:T(8,128)S(1)}, f32[32,2,2048]{2,0,1:T(8,128)S(1)}, u32[]{:S(2)}, u32[]{:S(2)}) collective-permute-start(f32[32,2,2048]{2,0,1:T(8,128)S(1)} %fusion.17), channel_id=1, source_target_pairs={{0,1},{1,2},{2,3},{3,4},{4,5},{5,6},{6,7},{7,0},{8,9},{9,10},{10,1... | collective-permute-start | bytes 1572872 | tf_op jit(solution)/shard_map/ppermute | solution.py:43
  44.6 14.1 %collective-permute-start.6 = (f32[32,2,2048]{2,0,1:T(8,128)S(1)}, f32[32,2,2048]{2,0,1:T(8,128)S(1)}, u32[]{:S(2)}, u32[]{:S(2)}) collective-permute-start(f32[32,2,2048]{2,0,1:T(8,128)S(1)} %fusion.17), channel_id=1, source_target_pairs={{1,0},{2,1},{3,2},{4,3},{5,4},{6,5},{7,6},{0,7},{9,8},{10,9},{11,1... | collective-permute-start | bytes 1572872 | tf_op jit(solution)/shard_map/ppermute | solution.py:44
  73.6 5.9 %collective-permute-start.8 = (f32[129,128]{1,0:T(8,128)S(1)}, f32[129,128]{1,0:T(8,128)S(1)}, u32[]{:S(2)}, u32[]{:S(2)}) collective-permute-start(f32[129,128]{1,0:T(8,128)S(1)} %pad_maximum_fusion.8), channel_id=1, source_target_pairs={{0,2},{1,3},{2,4},{3,5},{4,6},{5,7},{6,0},{7,1},{8,10},{9,11},{10,... | collective-permute-start | bytes 198152 | tf_op jit(solution)/shard_map/ppermute | solution.py:33
  77.5 5.8 %collective-permute-start.11 = (f32[129,128]{1,0:T(8,128)S(1)}, f32[129,128]{1,0:T(8,128)S(1)}, u32[]{:S(2)}, u32[]{:S(2)}) collective-permute-start(f32[129,128]{1,0:T(8,128)S(1)} %pad_maximum_fusion.8), channel_id=1, source_target_pairs={{0,6},{1,7},{2,0},{3,1},{4,2},{5,3},{6,4},{7,5},{8,14},{9,15},{10,... | collective-permute-start | bytes 198152 | tf_op jit(solution)/shard_map/ppermute | solution.py:33
  77.5 4.4 %collective-permute-start.10 = (f32[129,128]{1,0:T(8,128)S(1)}, f32[129,128]{1,0:T(8,128)S(1)}, u32[]{:S(2)}, u32[]{:S(2)}) collective-permute-start(f32[129,128]{1,0:T(8,128)S(1)} %pad_maximum_fusion.8), channel_id=1, source_target_pairs={{0,7},{1,0},{2,1},{3,2},{4,3},{5,4},{6,5},{7,6},{8,15},{9,8},{10,9... | collective-permute-start | bytes 198152 | tf_op jit(solution)/shard_map/ppermute | solution.py:33
  77.5 4.4 %collective-permute-start.9 = (f32[129,128]{1,0:T(8,128)S(1)}, f32[129,128]{1,0:T(8,128)S(1)}, u32[]{:S(2)}, u32[]{:S(2)}) collective-permute-start(f32[129,128]{1,0:T(8,128)S(1)} %pad_maximum_fusion.8), channel_id=1, source_target_pairs={{0,1},{1,2},{2,3},{3,4},{4,5},{5,6},{6,7},{7,0},{8,9},{9,10},{10,1... | collective-permute-start | bytes 198152 | tf_op jit(solution)/shard_map/ppermute | solution.py:33
  97.5 5.6 %collective-permute-start.12 = (f32[128,33]{0,1:T(8,128)S(1)}, f32[128,33]{0,1:T(8,128)S(1)}, u32[]{:S(2)}, u32[]{:S(2)}) collective-permute-start(f32[128,33]{0,1:T(8,128)S(1)} %pad_maximum_fusion.11), channel_id=1, source_target_pairs={{0,2},{1,3},{2,4},{3,5},{4,6},{5,7},{6,0},{7,1},{8,10},{9,11},{10,... | collective-permute-start | bytes 50696 | tf_op jit(solution)/shard_map/ppermute | solution.py:33
  102.3 4.8 %collective-permute-start.15 = (f32[128,33]{0,1:T(8,128)S(1)}, f32[128,33]{0,1:T(8,128)S(1)}, u32[]{:S(2)}, u32[]{:S(2)}) collective-permute-start(f32[128,33]{0,1:T(8,128)S(1)} %pad_maximum_fusion.11), channel_id=1, source_target_pairs={{0,6},{1,7},{2,0},{3,1},{4,2},{5,3},{6,4},{7,5},{8,14},{9,15},{10,... | collective-permute-start | bytes 50696 | tf_op jit(solution)/shard_map/ppermute | solution.py:33
  102.4 3.5 %collective-permute-start.14 = (f32[128,33]{0,1:T(8,128)S(1)}, f32[128,33]{0,1:T(8,128)S(1)}, u32[]{:S(2)}, u32[]{:S(2)}) collective-permute-start(f32[128,33]{0,1:T(8,128)S(1)} %pad_maximum_fusion.11), channel_id=1, source_target_pairs={{0,7},{1,0},{2,1},{3,2},{4,3},{5,4},{6,5},{7,6},{8,15},{9,8},{10,9... | collective-permute-start | bytes 50696 | tf_op jit(solution)/shard_map/ppermute | solution.py:33
  107.7 3.9 %collective-permute-start.16 = (f32[128,33]{0,1:T(8,128)S(1)}, f32[128,33]{0,1:T(8,128)S(1)}, u32[]{:S(2)}, u32[]{:S(2)}) collective-permute-start(f32[128,33]{0,1:T(8,128)S(1)} %pad_maximum_fusion.12), channel_id=1, source_target_pairs={{0,2},{1,3},{2,4},{3,5},{4,6},{5,7},{6,0},{7,1},{8,10},{9,11},{10,... | collective-permute-start | bytes 50696 | tf_op jit(solution)/shard_map/ppermute | solution.py:33
  110.2 4.8 %collective-permute-start.19 = (f32[128,33]{0,1:T(8,128)S(1)}, f32[128,33]{0,1:T(8,128)S(1)}, u32[]{:S(2)}, u32[]{:S(2)}) collective-permute-start(f32[128,33]{0,1:T(8,128)S(1)} %pad_maximum_fusion.12), channel_id=1, source_target_pairs={{0,6},{1,7},{2,0},{3,1},{4,2},{5,3},{6,4},{7,5},{8,14},{9,15},{10,... | collective-permute-start | bytes 50696 | tf_op jit(solution)/shard_map/ppermute | solution.py:33
  110.2 3.5 %collective-permute-start.18 = (f32[128,33]{0,1:T(8,128)S(1)}, f32[128,33]{0,1:T(8,128)S(1)}, u32[]{:S(2)}, u32[]{:S(2)}) collective-permute-start(f32[128,33]{0,1:T(8,128)S(1)} %pad_maximum_fusion.12), channel_id=1, source_target_pairs={{0,7},{1,0},{2,1},{3,2},{4,3},{5,4},{6,5},{7,6},{8,15},{9,8},{10,9... | collective-permute-start | bytes 50696 | tf_op jit(solution)/shard_map/ppermute | solution.py:33
  115.5 3.9 %collective-permute-start.20 = (f32[128,33]{0,1:T(8,128)S(1)}, f32[128,33]{0,1:T(8,128)S(1)}, u32[]{:S(2)}, u32[]{:S(2)}) collective-permute-start(f32[128,33]{0,1:T(8,128)S(1)} %pad_maximum_fusion.13), channel_id=1, source_target_pairs={{0,2},{1,3},{2,4},{3,5},{4,6},{5,7},{6,0},{7,1},{8,10},{9,11},{10,... | collective-permute-start | bytes 50696 | tf_op jit(solution)/shard_map/ppermute | solution.py:33
  118.0 4.8 %collective-permute-start.23 = (f32[128,33]{0,1:T(8,128)S(1)}, f32[128,33]{0,1:T(8,128)S(1)}, u32[]{:S(2)}, u32[]{:S(2)}) collective-permute-start(f32[128,33]{0,1:T(8,128)S(1)} %pad_maximum_fusion.13), channel_id=1, source_target_pairs={{0,6},{1,7},{2,0},{3,1},{4,2},{5,3},{6,4},{7,5},{8,14},{9,15},{10,... | collective-permute-start | bytes 50696 | tf_op jit(solution)/shard_map/ppermute | solution.py:33
  118.1 3.5 %collective-permute-start.22 = (f32[128,33]{0,1:T(8,128)S(1)}, f32[128,33]{0,1:T(8,128)S(1)}, u32[]{:S(2)}, u32[]{:S(2)}) collective-permute-start(f32[128,33]{0,1:T(8,128)S(1)} %pad_maximum_fusion.13), channel_id=1, source_target_pairs={{0,7},{1,0},{2,1},{3,2},{4,3},{5,4},{6,5},{7,6},{8,15},{9,8},{10,9... | collective-permute-start | bytes 50696 | tf_op jit(solution)/shard_map/ppermute | solution.py:33
  123.3 3.9 %collective-permute-start.24 = (f32[128,33]{0,1:T(8,128)S(1)}, f32[128,33]{0,1:T(8,128)S(1)}, u32[]{:S(2)}, u32[]{:S(2)}) collective-permute-start(f32[128,33]{0,1:T(8,128)S(1)} %pad_maximum_fusion.14), channel_id=1, source_target_pairs={{0,2},{1,3},{2,4},{3,5},{4,6},{5,7},{6,0},{7,1},{8,10},{9,11},{10,... | collective-permute-start | bytes 50696 | tf_op jit(solution)/shard_map/ppermute | solution.py:33
  125.8 4.8 %collective-permute-start.27 = (f32[128,33]{0,1:T(8,128)S(1)}, f32[128,33]{0,1:T(8,128)S(1)}, u32[]{:S(2)}, u32[]{:S(2)}) collective-permute-start(f32[128,33]{0,1:T(8,128)S(1)} %pad_maximum_fusion.14), channel_id=1, source_target_pairs={{0,6},{1,7},{2,0},{3,1},{4,2},{5,3},{6,4},{7,5},{8,14},{9,15},{10,... | collective-permute-start | bytes 50696 | tf_op jit(solution)/shard_map/ppermute | solution.py:33
  131.2 3.9 %collective-permute-start.28 = (f32[128,33]{0,1:T(8,128)S(1)}, f32[128,33]{0,1:T(8,128)S(1)}, u32[]{:S(2)}, u32[]{:S(2)}) collective-permute-start(f32[128,33]{0,1:T(8,128)S(1)} %pad_maximum_fusion.15), channel_id=1, source_target_pairs={{0,2},{1,3},{2,4},{3,5},{4,6},{5,7},{6,0},{7,1},{8,10},{9,11},{10,... | collective-permute-start | bytes 50696 | tf_op jit(solution)/shard_map/ppermute | solution.py:33
  133.7 4.8 %collective-permute-start.31 = (f32[128,33]{0,1:T(8,128)S(1)}, f32[128,33]{0,1:T(8,128)S(1)}, u32[]{:S(2)}, u32[]{:S(2)}) collective-permute-start(f32[128,33]{0,1:T(8,128)S(1)} %pad_maximum_fusion.15), channel_id=1, source_target_pairs={{0,6},{1,7},{2,0},{3,1},{4,2},{5,3},{6,4},{7,5},{8,14},{9,15},{10,... | collective-permute-start | bytes 50696 | tf_op jit(solution)/shard_map/ppermute | solution.py:33
  139.0 3.8 %collective-permute-start.32 = (f32[1,128,32]{1,2,0:T(8,128)S(1)}, f32[1,128,32]{1,2,0:T(8,128)S(1)}, u32[]{:S(2)}, u32[]{:S(2)}) collective-permute-start(f32[1,128,32]{1,2,0:T(8,128)S(1)} %bitcast.129), channel_id=1, source_target_pairs={{0,8},{8,0},{16,24},{24,16},{1,9},{9,1},{17,25},{25,17},{2,10},{10... | collective-permute-start | bytes 49160 | tf_op jit(solution)/shard_map/ppermute | solution.py:23
  142.8 9.3 %collective-permute-start.33 = (f32[2,128,32]{1,2,0:T(8,128)S(1)}, f32[2,128,32]{1,2,0:T(8,128)S(1)}, u32[]{:S(2)}, u32[]{:S(2)}) collective-permute-start(f32[2,128,32]{1,2,0:T(8,128)S(1)} %get-tuple-element.71), channel_id=1, source_target_pairs={{0,16},{8,24},{16,0},{24,8},{1,17},{9,25},{17,1},{25,9},{2,18},{10... | collective-permute-start | bytes 98312 | tf_op jit(solution)/shard_map/ppermute | solution.py:23
  148.6 17.4 %all-to-all-start = ((f32[4,1,32768]{2,1,0:T(1,128)}), f32[4,1,32768]{2,1,0:T(1,128)S(1)}, u32[]{:S(2)}, u32[]{:S(2)}) async-start(f32[4,1,32768]{2,1,0:T(1,128)} %reshape.51), calls=%async_computation | async-start | bytes 1048576 | tf_op jit(solution)/shard_map/all_to_all | solution.py:144
  152.2 4.5 %collective-permute-start.34 = (f32[128,128]{0,1:T(8,128)S(1)}, f32[128,128]{0,1:T(8,128)S(1)}, u32[]{:S(2)}, u32[]{:S(2)}) collective-permute-start(f32[128,128]{0,1:T(8,128)S(1)} %bitcast.124), channel_id=1, source_target_pairs={{0,2},{1,3},{2,4},{3,5},{4,6},{5,7},{6,0},{7,1},{8,10},{9,11},{10,... | collective-permute-start | bytes 196616 | tf_op jit(solution)/shard_map/ppermute | solution.py:33
  154.9 5.7 %collective-permute-start.37 = (f32[128,128]{0,1:T(8,128)S(1)}, f32[128,128]{0,1:T(8,128)S(1)}, u32[]{:S(2)}, u32[]{:S(2)}) collective-permute-start(f32[128,128]{0,1:T(8,128)S(1)} %bitcast.125), channel_id=1, source_target_pairs={{0,6},{1,7},{2,0},{3,1},{4,2},{5,3},{6,4},{7,5},{8,14},{9,15},{10,... | collective-permute-start | bytes 196616 | tf_op jit(solution)/shard_map/ppermute | solution.py:33
  154.9 4.7 %collective-permute-start.36 = (f32[128,128]{0,1:T(8,128)S(1)}, f32[128,128]{0,1:T(8,128)S(1)}, u32[]{:S(2)}, u32[]{:S(2)}) collective-permute-start(f32[128,128]{0,1:T(8,128)S(1)} %bitcast.126), channel_id=1, source_target_pairs={{0,7},{1,0},{2,1},{3,2},{4,3},{5,4},{6,5},{7,6},{8,15},{9,8},{10,9... | collective-permute-start | bytes 196616 | tf_op jit(solution)/shard_map/ppermute | solution.py:33
  155.0 4.6 %collective-permute-start.35 = (f32[128,128]{0,1:T(8,128)S(1)}, f32[128,128]{0,1:T(8,128)S(1)}, u32[]{:S(2)}, u32[]{:S(2)}) collective-permute-start(f32[128,128]{0,1:T(8,128)S(1)} %bitcast.127), channel_id=1, source_target_pairs={{0,1},{1,2},{2,3},{3,4},{4,5},{5,6},{6,7},{7,0},{8,9},{9,10},{10,1... | collective-permute-start | bytes 196616 | tf_op jit(solution)/shard_map/ppermute | solution.py:33
  (12 other events, 191.8 us)
